TPU v7x, 32 devices: a whole 2x2x4 slice. The times are simulated.
32 devices in a mesh: arrays: 2 (over y), tm: 8 (over z, x), chan: 2 (over core).
Axes of the slice: x: 2, y: 2, z: 4, core: 2. Of those that a mesh axis runs over, the one named last changes fastest.
Arguments:
- spectra: bfloat16 [128, 256, 2, 128], P(('arrays', 'tm'), 'chan'), parts along dimension 0, may hold values from -40 to 40
- offsets: int32 [128], P(('arrays', 'tm')), parts along dimension 0, may hold values from 0 to 63
- channel_group: int32 [512], P(('arrays', 'chan')), parts along dimension 0, may hold values from 0 to 7
Outputs:
- stack: float32 [128, 48, 128], P(('arrays', 'tm', 'chan')), parts along dimension 0
There are 2 independent parts, one for each index of `arrays`. A program takes and returns all parts, laid end to end along the dimension named above; each array names one. Nothing has to cross between parts.
All inputs are finite; a program needn't handle non-finite values.
Results may differ from a plain program's by a relative error of at most 0.0075.
Values may be sent and summed in bfloat16 or wider, within the bound.
A program may use at most 64 MiB of HBM per device.

v0:
```python
import math

import jax
import jax.numpy as jnp
from jax import lax
from jax.sharding import PartitionSpec as P

LAGS = 128
GROUPS = 8
SPAN = 6


epsilon = 1e-05


def shifted(value, axis, steps):
    count = lax.axis_size(axis)
    initial, last = (max(0, -steps), min(count, count - steps))
    return lax.ppermute(value, axis, [(source, source + steps) for source in range(initial, last)])


def lag_table(freq_bins, lag_count):
    frequency = jnp.arange(freq_bins, dtype=jnp.int32)[:, None]
    lag_shift = jnp.arange(lag_count, dtype=jnp.int32)[None, :] - lag_count // 2
    phase_turns = jnp.mod(frequency * lag_shift, 2 * freq_bins).astype(jnp.float32)
    phase_angle = jnp.pi * phase_turns / freq_bins
    normaliser = 1.0 / math.sqrt(freq_bins)
    lag_rows = jnp.concatenate(
        [jnp.cos(phase_angle) * normaliser, -jnp.sin(phase_angle) * normaliser], axis=0
    )
    return lag_rows.astype(jnp.bfloat16)


def align_spectra(spectra, offsets, scales):
    freq_bins = spectra.shape[3]
    frequency = jnp.arange(freq_bins, dtype=jnp.int32)[None, :]
    phase_turns = jnp.mod(offsets[:, None] * frequency, 2 * freq_bins).astype(jnp.float32)
    phase_angle = jnp.pi * phase_turns / freq_bins
    cosine = jnp.cos(phase_angle)[:, None, :]
    sine_part = jnp.sin(phase_angle)[:, None, :]
    real_part = spectra[:, :, 0, :].astype(jnp.float32)
    imag_part = spectra[:, :, 1, :].astype(jnp.float32)
    weight = scales[:, :, None]
    out_real = weight * (real_part * cosine + imag_part * sine_part)
    out_imag = weight * (imag_part * cosine - real_part * sine_part)
    return jnp.stack([out_real, out_imag], axis=2).astype(jnp.bfloat16)


def window_terms(current, band_rows, lag_rows):
    left_real = current[None, :, 0, :].astype(jnp.float32)
    left_imag = current[None, :, 1, :].astype(jnp.float32)
    right_real = band_rows[:, :, 0, :].astype(jnp.float32)
    right_imag = band_rows[:, :, 1, :].astype(jnp.float32)
    prod_real = left_real * right_real + left_imag * right_imag
    prod_imag = left_imag * right_real - left_real * right_imag
    cross_spec = jnp.stack([prod_real, prod_imag], axis=2).astype(jnp.bfloat16)
    flattened = cross_spec.reshape(band_rows.shape[0] * band_rows.shape[1], 2 * band_rows.shape[3])
    lagged = jnp.dot(flattened, lag_rows, preferred_element_type=jnp.float32)
    lagged = lagged.reshape(band_rows.shape[0], band_rows.shape[1], lag_rows.shape[1])
    return jnp.sum(lagged * lagged, axis=1)


def shards(spectra, offsets, channel_group):
    windows = spectra.shape[0]
    local_chans = spectra.shape[1]
    freq_bins = spectra.shape[3]
    chan_count = lax.axis_size("chan")
    channels = local_chans * chan_count
    onehot = (channel_group[:, None] == jnp.arange(GROUPS, dtype=jnp.int32)[None, :]).astype(
        jnp.float32
    )
    chan_power = jnp.sum(jnp.square(spectra.astype(jnp.float32)), axis=(2, 3))
    partial_value = jnp.dot(chan_power, onehot, precision=lax.Precision.HIGHEST)
    group_total = lax.psum(partial_value, "chan")
    energy = group_total * (GROUPS / (freq_bins * channels))
    scales = jnp.dot(lax.rsqrt(energy + epsilon), onehot.T, precision=lax.Precision.HIGHEST)
    aligned = align_spectra(spectra, offsets, scales)
    earlier = []
    carried = aligned
    for distance in range(SPAN):
        carried = shifted(carried, "tm", 1)
        earlier.append(carried)
    buffer = jnp.concatenate(earlier[::-1] + [aligned], axis=0)
    lag_rows = lag_table(freq_bins, LAGS)
    band_len = SPAN * windows

    def one_window(window):
        current = lax.dynamic_index_in_dim(aligned, window, 0, keepdims=False)
        band_rows = lax.dynamic_slice_in_dim(buffer, window, band_len, 0)
        return window_terms(current, band_rows, lag_rows) * (1.0 / channels)

    return lax.psum_scatter(
        lax.map(
            one_window, jnp.arange(lax.axis_size("chan") * (windows // chan_count), dtype=jnp.int32)
        ).astype(jnp.bfloat16),
        "chan",
        scatter_dimension=0,
        tiled=True,
    ).astype(jnp.float32)


def solution(mesh):
    placed = (P(("arrays", "tm"), "chan", None, None), P(("arrays", "tm")), P(("arrays", "chan")))
    return jax.shard_map(
        shards,
        mesh=mesh,
        in_specs=placed,
        out_specs=P(("arrays", "tm", "chan"), None, None),
        check_vma=False,
    )
```

profile of v0, /device:TPU:0, one launch (start us, length us, event | category | flops | bytes accessed | tf_op | source)
XLA Modules:
  0.0 234.6 jit_solution(17120011980369295450)
XLA Ops:
  6.5 2.3 fusion.38
  8.8 3.1 %multiply_reduce_fusion.1 = f32[8,128]{1,0:T(8,128)S(1)} fusion(bf16[8,128,2,128]{3,2,1,0:T(2,128)(2,1)} %param.5), kind=kLoop, calls=%fused_computation.17 | loop fusion | flops 785408 | bytes 528384 | tf_op jit(solution)/shard_map/reduce_sum | solution.py:72
  11.9 0.8 fusion.33
  12.7 0.8 fusion.19
  13.6 2.6 %psum.7 = f32[8,8]{1,0:T(8,128)S(1)} all-reduce(f32[8,8]{1,0:T(8,128)S(1)} %fusion.19), channel_id=1, replica_groups=mesh['arrays'=2,'tm'=8,'chan'=2] {'chan'}, use_global_device_ids=true, to_apply=%region_1.0 | all-reduce | flops 64 | bytes 512 | tf_op jit(solution)/shard_map/psum | solution.py:74
  16.2 0.8 fusion.18
  17.5 4.7 %collective-permute-start = (bf16[8,128,2,128]{3,1,2,0:T(8,128)(2,1)S(1)}, bf16[8,128,2,128]{3,1,2,0:T(8,128)(2,1)S(1)}, u32[]{:S(2)}, u32[]{:S(2)}) collective-permute-start(bf16[8,128,2,128]{3,1,2,0:T(8,128)(2,1)S(1)} %pad_maximum_fusion.1), channel_id=1, source_target_pairs={{0,2},{2,4},{4,6},{6,8},{8,10},{10,12},{12,14},{1,3},{3,5},{5,7},{... | collective-permute-start | bytes 1572872 | tf_op jit(solution)/shard_map/ppermute | solution.py:19
  22.2 11.5 %collective-permute-done = bf16[8,128,2,128]{3,1,2,0:T(8,128)(2,1)S(1)} collective-permute-done((bf16[8,128,2,128]{3,1,2,0:T(8,128)(2,1)S(1)}, bf16[8,128,2,128]{3,1,2,0:T(8,128)(2,1)S(1)}, u32[]{:S(2)}, u32[]{:S(2)}) %collective-permute-start) | collective-permute-done | bytes 524320 | tf_op jit(solution)/shard_map/ppermute | solution.py:19
  33.7 4.4 %collective-permute-start.1 = (bf16[8,128,2,128]{3,1,2,0:T(8,128)(2,1)S(1)}, bf16[8,128,2,128]{3,1,2,0:T(8,128)(2,1)S(1)}, u32[]{:S(2)}, u32[]{:S(2)}) collective-permute-start(bf16[8,128,2,128]{3,1,2,0:T(8,128)(2,1)S(1)} %collective-permute-done), channel_id=1, source_target_pairs={{0,2},{2,4},{4,6},{6,8},{8,10},{10,12},{12,14},{1,3},{3,5},{5,7},{... | collective-permute-start | bytes 1572872 | tf_op jit(solution)/shard_map/ppermute | solution.py:19
  38.1 10.6 %collective-permute-done.1 = bf16[8,128,2,128]{3,1,2,0:T(8,128)(2,1)S(1)} collective-permute-done((bf16[8,128,2,128]{3,1,2,0:T(8,128)(2,1)S(1)}, bf16[8,128,2,128]{3,1,2,0:T(8,128)(2,1)S(1)}, u32[]{:S(2)}, u32[]{:S(2)}) %collective-permute-start.1) | collective-permute-done | bytes 524320 | tf_op jit(solution)/shard_map/ppermute | solution.py:19
  48.7 4.4 %collective-permute-start.2 = (bf16[8,128,2,128]{3,1,2,0:T(8,128)(2,1)S(1)}, bf16[8,128,2,128]{3,1,2,0:T(8,128)(2,1)S(1)}, u32[]{:S(2)}, u32[]{:S(2)}) collective-permute-start(bf16[8,128,2,128]{3,1,2,0:T(8,128)(2,1)S(1)} %collective-permute-done.1), channel_id=1, source_target_pairs={{0,2},{2,4},{4,6},{6,8},{8,10},{10,12},{12,14},{1,3},{3,5},{5,7},{... | collective-permute-start | bytes 1572872 | tf_op jit(solution)/shard_map/ppermute | solution.py:19
  53.1 9.7 %collective-permute-done.2 = bf16[8,128,2,128]{3,1,2,0:T(8,128)(2,1)S(1)} collective-permute-done((bf16[8,128,2,128]{3,1,2,0:T(8,128)(2,1)S(1)}, bf16[8,128,2,128]{3,1,2,0:T(8,128)(2,1)S(1)}, u32[]{:S(2)}, u32[]{:S(2)}) %collective-permute-start.2) | collective-permute-done | bytes 524320 | tf_op jit(solution)/shard_map/ppermute | solution.py:19
  62.9 5.3 %collective-permute-start.3 = (bf16[8,128,2,128]{3,1,2,0:T(8,128)(2,1)S(1)}, bf16[8,128,2,128]{3,1,2,0:T(8,128)(2,1)S(1)}, u32[]{:S(2)}, u32[]{:S(2)}) collective-permute-start(bf16[8,128,2,128]{3,1,2,0:T(8,128)(2,1)S(1)} %collective-permute-done.2), channel_id=1, source_target_pairs={{0,2},{2,4},{4,6},{6,8},{8,10},{10,12},{12,14},{1,3},{3,5},{5,7},{... | collective-permute-start | bytes 1572872 | tf_op jit(solution)/shard_map/ppermute | solution.py:19
  68.2 8.9 %collective-permute-done.3 = bf16[8,128,2,128]{3,1,2,0:T(8,128)(2,1)S(1)} collective-permute-done((bf16[8,128,2,128]{3,1,2,0:T(8,128)(2,1)S(1)}, bf16[8,128,2,128]{3,1,2,0:T(8,128)(2,1)S(1)}, u32[]{:S(2)}, u32[]{:S(2)}) %collective-permute-start.3) | collective-permute-done | bytes 524320 | tf_op jit(solution)/shard_map/ppermute | solution.py:19
  77.1 6.1 %collective-permute-start.4 = (bf16[8,128,2,128]{3,1,2,0:T(8,128)(2,1)S(1)}, bf16[8,128,2,128]{3,1,2,0:T(8,128)(2,1)}, u32[]{:S(2)}, u32[]{:S(2)}) collective-permute-start(bf16[8,128,2,128]{3,1,2,0:T(8,128)(2,1)S(1)} %collective-permute-done.3), channel_id=1, source_target_pairs={{0,2},{2,4},{4,6},{6,8},{8,10},{10,12},{12,14},{1,3},{3,5},{5,7},{... | collective-permute-start | bytes 1572872 | tf_op jit(solution)/shard_map/ppermute | solution.py:19
  83.1 7.3 %collective-permute-done.4 = bf16[8,128,2,128]{3,1,2,0:T(8,128)(2,1)} collective-permute-done((bf16[8,128,2,128]{3,1,2,0:T(8,128)(2,1)S(1)}, bf16[8,128,2,128]{3,1,2,0:T(8,128)(2,1)}, u32[]{:S(2)}, u32[]{:S(2)}) %collective-permute-start.4) | collective-permute-done | bytes 524320 | tf_op jit(solution)/shard_map/ppermute | solution.py:19
  90.4 6.1 %collective-permute-start.5 = (bf16[8,128,2,128]{3,1,2,0:T(8,128)(2,1)}, bf16[8,128,2,128]{3,1,2,0:T(8,128)(2,1)}, u32[]{:S(2)}, u32[]{:S(2)}) collective-permute-start(bf16[8,128,2,128]{3,1,2,0:T(8,128)(2,1)} %collective-permute-done.4), channel_id=1, source_target_pairs={{0,2},{2,4},{4,6},{6,8},{8,10},{10,12},{12,14},{1,3},{3,5},{5,7},{... | collective-permute-start | bytes 1572872 | tf_op jit(solution)/shard_map/ppermute | solution.py:19
  96.8 6.4 %collective-permute-done.5 = bf16[8,128,2,128]{3,1,2,0:T(8,128)(2,1)} collective-permute-done((bf16[8,128,2,128]{3,1,2,0:T(8,128)(2,1)}, bf16[8,128,2,128]{3,1,2,0:T(8,128)(2,1)}, u32[]{:S(2)}, u32[]{:S(2)}) %collective-permute-start.5) | collective-permute-done | bytes 524320 | tf_op jit(solution)/shard_map/ppermute | solution.py:19
  103.2 1.1 constant_dynamic-update-slice_fusion.6
  104.3 1.1 constant_dynamic-update-slice_fusion.5
  105.8 1.8 copy-done
  107.6 106.2 %while.10 = (s32[]{:T(128)}, bf16[8,48,128]{2,1,0:T(8,128)(2,1)S(1)}, s32[8]{0:T(128)S(1)}, bf16[8,128,2,128]{3,1,2,0:T(8,128)(2,1)S(1)}, bf16[56,128,2,128]{3,1...) while((s32[]{:T(128)}, ...), condition=%wide.region_4.5_spmd, body=%wide.region_2.4_spmd.sunk | while | flops 413696000 | bytes 26812680 | solution.py:93
  111.4 3.3 %fusion.48 = (bf16[48,128,1,128]{3,1,2,0:T(8,128)(2,1)S(1)}, bf16[48,128,1,128]{3,1,2,0:T(8,128)(2,1)S(1)}) fusion(f32[128,128]{1,0:T(8,128)S(1)} %get-tuple-element.103, f32[128,128]{1,0:T(8,128)S(1)} %get-tuple-element.104, bf16[56,128,2,128]{3,1,2,0:T(8,128)(2,1)} %get-tuple-element.133, s32[]{:T(128)S(6)} %select_n.52, s32[]{:T(128)S(6)} %add.104), kind=kLoop, calls=%fused_computation.5.clone.1 | loop fusion | flops 7864320 | bytes 6422536 | tf_op jit(solution)/shard_map/convert.2
  115.0 2.8 %copy.22 = bf16[48,128,2,128]{1,3,2,0:T(8,128)(2,1)} copy(bf16[48,128,2,128]{3,1,2,0:T(8,128)(2,1)S(1)} %pad_maximum_fusion.4) | data formatting | bytes 6291456 | tf_op jit(solution)/shard_map/while/body/eval_jaxpr/stack | solution.py:56
  117.8 3.0 %multiply_reduce_fusion.3 = f32[48,128]{1,0:T(8,128)S(1)} fusion(bf16[48,128,256]{1,2,0:T(8,128)(2,1)} %bitcast.35, bf16[256,128]{1,0:T(8,128)(2,1)S(1)} %get-tuple-element.134), kind=kOutput, calls=%fused_computation.9.clone.1 | convolution fusion | flops 404219904 | bytes 3235840 | tf_op jit(solution)/shard_map/while/body/eval_jaxpr/dot_general | solution.py:58
  124.7 3.3 %fusion.48 = (bf16[48,128,1,128]{3,1,2,0:T(8,128)(2,1)S(1)}, bf16[48,128,1,128]{3,1,2,0:T(8,128)(2,1)S(1)}) fusion(f32[128,128]{1,0:T(8,128)S(1)} %get-tuple-element.103, f32[128,128]{1,0:T(8,128)S(1)} %get-tuple-element.104, bf16[56,128,2,128]{3,1,2,0:T(8,128)(2,1)} %get-tuple-element.133, s32[]{:T(128)S(6)} %select_n.52, s32[]{:T(128)S(6)} %add.104), kind=kLoop, calls=%fused_computation.5.clone.1 | loop fusion | flops 7864320 | bytes 6422536 | tf_op jit(solution)/shard_map/convert.2
  128.3 2.8 %copy.22 = bf16[48,128,2,128]{1,3,2,0:T(8,128)(2,1)} copy(bf16[48,128,2,128]{3,1,2,0:T(8,128)(2,1)S(1)} %pad_maximum_fusion.4) | data formatting | bytes 6291456 | tf_op jit(solution)/shard_map/while/body/eval_jaxpr/stack | solution.py:56
  131.1 3.0 %multiply_reduce_fusion.3 = f32[48,128]{1,0:T(8,128)S(1)} fusion(bf16[48,128,256]{1,2,0:T(8,128)(2,1)} %bitcast.35, bf16[256,128]{1,0:T(8,128)(2,1)S(1)} %get-tuple-element.134), kind=kOutput, calls=%fused_computation.9.clone.1 | convolution fusion | flops 404219904 | bytes 3235840 | tf_op jit(solution)/shard_map/while/body/eval_jaxpr/dot_general | solution.py:58
  137.9 3.3 %fusion.48 = (bf16[48,128,1,128]{3,1,2,0:T(8,128)(2,1)S(1)}, bf16[48,128,1,128]{3,1,2,0:T(8,128)(2,1)S(1)}) fusion(f32[128,128]{1,0:T(8,128)S(1)} %get-tuple-element.103, f32[128,128]{1,0:T(8,128)S(1)} %get-tuple-element.104, bf16[56,128,2,128]{3,1,2,0:T(8,128)(2,1)} %get-tuple-element.133, s32[]{:T(128)S(6)} %select_n.52, s32[]{:T(128)S(6)} %add.104), kind=kLoop, calls=%fused_computation.5.clone.1 | loop fusion | flops 7864320 | bytes 6422536 | tf_op jit(solution)/shard_map/convert.2
  141.5 2.8 %copy.22 = bf16[48,128,2,128]{1,3,2,0:T(8,128)(2,1)} copy(bf16[48,128,2,128]{3,1,2,0:T(8,128)(2,1)S(1)} %pad_maximum_fusion.4) | data formatting | bytes 6291456 | tf_op jit(solution)/shard_map/while/body/eval_jaxpr/stack | solution.py:56
  144.4 3.0 %multiply_reduce_fusion.3 = f32[48,128]{1,0:T(8,128)S(1)} fusion(bf16[48,128,256]{1,2,0:T(8,128)(2,1)} %bitcast.35, bf16[256,128]{1,0:T(8,128)(2,1)S(1)} %get-tuple-element.134), kind=kOutput, calls=%fused_computation.9.clone.1 | convolution fusion | flops 404219904 | bytes 3235840 | tf_op jit(solution)/shard_map/while/body/eval_jaxpr/dot_general | solution.py:58
  151.2 3.3 %fusion.48 = (bf16[48,128,1,128]{3,1,2,0:T(8,128)(2,1)S(1)}, bf16[48,128,1,128]{3,1,2,0:T(8,128)(2,1)S(1)}) fusion(f32[128,128]{1,0:T(8,128)S(1)} %get-tuple-element.103, f32[128,128]{1,0:T(8,128)S(1)} %get-tuple-element.104, bf16[56,128,2,128]{3,1,2,0:T(8,128)(2,1)} %get-tuple-element.133, s32[]{:T(128)S(6)} %select_n.52, s32[]{:T(128)S(6)} %add.104), kind=kLoop, calls=%fused_computation.5.clone.1 | loop fusion | flops 7864320 | bytes 6422536 | tf_op jit(solution)/shard_map/convert.2
  154.8 2.8 %copy.22 = bf16[48,128,2,128]{1,3,2,0:T(8,128)(2,1)} copy(bf16[48,128,2,128]{3,1,2,0:T(8,128)(2,1)S(1)} %pad_maximum_fusion.4) | data formatting | bytes 6291456 | tf_op jit(solution)/shard_map/while/body/eval_jaxpr/stack | solution.py:56
  157.6 3.0 %multiply_reduce_fusion.3 = f32[48,128]{1,0:T(8,128)S(1)} fusion(bf16[48,128,256]{1,2,0:T(8,128)(2,1)} %bitcast.35, bf16[256,128]{1,0:T(8,128)(2,1)S(1)} %get-tuple-element.134), kind=kOutput, calls=%fused_computation.9.clone.1 | convolution fusion | flops 404219904 | bytes 3235840 | tf_op jit(solution)/shard_map/while/body/eval_jaxpr/dot_general | solution.py:58
  164.5 3.3 %fusion.48 = (bf16[48,128,1,128]{3,1,2,0:T(8,128)(2,1)S(1)}, bf16[48,128,1,128]{3,1,2,0:T(8,128)(2,1)S(1)}) fusion(f32[128,128]{1,0:T(8,128)S(1)} %get-tuple-element.103, f32[128,128]{1,0:T(8,128)S(1)} %get-tuple-element.104, bf16[56,128,2,128]{3,1,2,0:T(8,128)(2,1)} %get-tuple-element.133, s32[]{:T(128)S(6)} %select_n.52, s32[]{:T(128)S(6)} %add.104), kind=kLoop, calls=%fused_computation.5.clone.1 | loop fusion | flops 7864320 | bytes 6422536 | tf_op jit(solution)/shard_map/convert.2
  168.1 2.8 %copy.22 = bf16[48,128,2,128]{1,3,2,0:T(8,128)(2,1)} copy(bf16[48,128,2,128]{3,1,2,0:T(8,128)(2,1)S(1)} %pad_maximum_fusion.4) | data formatting | bytes 6291456 | tf_op jit(solution)/shard_map/while/body/eval_jaxpr/stack | solution.py:56
  170.9 3.0 %multiply_reduce_fusion.3 = f32[48,128]{1,0:T(8,128)S(1)} fusion(bf16[48,128,256]{1,2,0:T(8,128)(2,1)} %bitcast.35, bf16[256,128]{1,0:T(8,128)(2,1)S(1)} %get-tuple-element.134), kind=kOutput, calls=%fused_computation.9.clone.1 | convolution fusion | flops 404219904 | bytes 3235840 | tf_op jit(solution)/shard_map/while/body/eval_jaxpr/dot_general | solution.py:58
  177.8 3.3 %fusion.48 = (bf16[48,128,1,128]{3,1,2,0:T(8,128)(2,1)S(1)}, bf16[48,128,1,128]{3,1,2,0:T(8,128)(2,1)S(1)}) fusion(f32[128,128]{1,0:T(8,128)S(1)} %get-tuple-element.103, f32[128,128]{1,0:T(8,128)S(1)} %get-tuple-element.104, bf16[56,128,2,128]{3,1,2,0:T(8,128)(2,1)} %get-tuple-element.133, s32[]{:T(128)S(6)} %select_n.52, s32[]{:T(128)S(6)} %add.104), kind=kLoop, calls=%fused_computation.5.clone.1 | loop fusion | flops 7864320 | bytes 6422536 | tf_op jit(solution)/shard_map/convert.2
  181.4 2.8 %copy.22 = bf16[48,128,2,128]{1,3,2,0:T(8,128)(2,1)} copy(bf16[48,128,2,128]{3,1,2,0:T(8,128)(2,1)S(1)} %pad_maximum_fusion.4) | data formatting | bytes 6291456 | tf_op jit(solution)/shard_map/while/body/eval_jaxpr/stack | solution.py:56
  184.2 3.0 %multiply_reduce_fusion.3 = f32[48,128]{1,0:T(8,128)S(1)} fusion(bf16[48,128,256]{1,2,0:T(8,128)(2,1)} %bitcast.35, bf16[256,128]{1,0:T(8,128)(2,1)S(1)} %get-tuple-element.134), kind=kOutput, calls=%fused_computation.9.clone.1 | convolution fusion | flops 404219904 | bytes 3235840 | tf_op jit(solution)/shard_map/while/body/eval_jaxpr/dot_general | solution.py:58
  191.0 3.3 %fusion.48 = (bf16[48,128,1,128]{3,1,2,0:T(8,128)(2,1)S(1)}, bf16[48,128,1,128]{3,1,2,0:T(8,128)(2,1)S(1)}) fusion(f32[128,128]{1,0:T(8,128)S(1)} %get-tuple-element.103, f32[128,128]{1,0:T(8,128)S(1)} %get-tuple-element.104, bf16[56,128,2,128]{3,1,2,0:T(8,128)(2,1)} %get-tuple-element.133, s32[]{:T(128)S(6)} %select_n.52, s32[]{:T(128)S(6)} %add.104), kind=kLoop, calls=%fused_computation.5.clone.1 | loop fusion | flops 7864320 | bytes 6422536 | tf_op jit(solution)/shard_map/convert.2
  194.6 2.8 %copy.22 = bf16[48,128,2,128]{1,3,2,0:T(8,128)(2,1)} copy(bf16[48,128,2,128]{3,1,2,0:T(8,128)(2,1)S(1)} %pad_maximum_fusion.4) | data formatting | bytes 6291456 | tf_op jit(solution)/shard_map/while/body/eval_jaxpr/stack | solution.py:56
  197.5 3.0 %multiply_reduce_fusion.3 = f32[48,128]{1,0:T(8,128)S(1)} fusion(bf16[48,128,256]{1,2,0:T(8,128)(2,1)} %bitcast.35, bf16[256,128]{1,0:T(8,128)(2,1)S(1)} %get-tuple-element.134), kind=kOutput, calls=%fused_computation.9.clone.1 | convolution fusion | flops 404219904 | bytes 3235840 | tf_op jit(solution)/shard_map/while/body/eval_jaxpr/dot_general | solution.py:58
  204.3 3.3 %fusion.48 = (bf16[48,128,1,128]{3,1,2,0:T(8,128)(2,1)S(1)}, bf16[48,128,1,128]{3,1,2,0:T(8,128)(2,1)S(1)}) fusion(f32[128,128]{1,0:T(8,128)S(1)} %get-tuple-element.103, f32[128,128]{1,0:T(8,128)S(1)} %get-tuple-element.104, bf16[56,128,2,128]{3,1,2,0:T(8,128)(2,1)} %get-tuple-element.133, s32[]{:T(128)S(6)} %select_n.52, s32[]{:T(128)S(6)} %add.104), kind=kLoop, calls=%fused_computation.5.clone.1 | loop fusion | flops 7864320 | bytes 6422536 | tf_op jit(solution)/shard_map/convert.2
  207.9 2.8 %copy.22 = bf16[48,128,2,128]{1,3,2,0:T(8,128)(2,1)} copy(bf16[48,128,2,128]{3,1,2,0:T(8,128)(2,1)S(1)} %pad_maximum_fusion.4) | data formatting | bytes 6291456 | tf_op jit(solution)/shard_map/while/body/eval_jaxpr/stack | solution.py:56
  210.7 3.0 %multiply_reduce_fusion.3 = f32[48,128]{1,0:T(8,128)S(1)} fusion(bf16[48,128,256]{1,2,0:T(8,128)(2,1)} %bitcast.35, bf16[256,128]{1,0:T(8,128)(2,1)S(1)} %get-tuple-element.134), kind=kOutput, calls=%fused_computation.9.clone.1 | convolution fusion | flops 404219904 | bytes 3235840 | tf_op jit(solution)/shard_map/while/body/eval_jaxpr/dot_general | solution.py:58
  214.4 11.9 %reduce-scatter.2.cloned.1.call-done = bf16[4,48,128]{2,1,0:T(8,128)(2,1)} async-done(((bf16[8,48,128]{2,1,0:T(8,128)(2,1)}), bf16[4,48,128]{2,1,0:T(8,128)(2,1)}) %reduce-scatter.2.cloned.1.call-update) | async-done | bytes 49168 | tf_op jit(solution)/shard_map/reduce_scatter | solution.py:92
  226.3 1.4 convert_element_type.81
  (89 shorter events, 9.9 us)
Async XLA Ops:
  6.5 219.8 %reduce-scatter.2.cloned.1.call-start = ((), (), s32[]{:S(2)}) async-start(), calls=%async_computation.1 | async-start | bytes 147456 | tf_op jit(solution)/shard_map/reduce_scatter | solution.py:92
  17.5 16.2 %collective-permute-start = (bf16[8,128,2,128]{3,1,2,0:T(8,128)(2,1)S(1)}, bf16[8,128,2,128]{3,1,2,0:T(8,128)(2,1)S(1)}, u32[]{:S(2)}, u32[]{:S(2)}) collective-permute-start(bf16[8,128,2,128]{3,1,2,0:T(8,128)(2,1)S(1)} %pad_maximum_fusion.1), channel_id=1, source_target_pairs={{0,2},{2,4},{4,6},{6,8},{8,10},{10,12},{12,14},{1,3},{3,5},{5,7},{... | collective-permute-start | bytes 1572872 | tf_op jit(solution)/shard_map/ppermute | solution.py:19
  33.7 15.0 %collective-permute-start.1 = (bf16[8,128,2,128]{3,1,2,0:T(8,128)(2,1)S(1)}, bf16[8,128,2,128]{3,1,2,0:T(8,128)(2,1)S(1)}, u32[]{:S(2)}, u32[]{:S(2)}) collective-permute-start(bf16[8,128,2,128]{3,1,2,0:T(8,128)(2,1)S(1)} %collective-permute-done), channel_id=1, source_target_pairs={{0,2},{2,4},{4,6},{6,8},{8,10},{10,12},{12,14},{1,3},{3,5},{5,7},{... | collective-permute-start | bytes 1572872 | tf_op jit(solution)/shard_map/ppermute | solution.py:19
  48.7 14.2 %collective-permute-start.2 = (bf16[8,128,2,128]{3,1,2,0:T(8,128)(2,1)S(1)}, bf16[8,128,2,128]{3,1,2,0:T(8,128)(2,1)S(1)}, u32[]{:S(2)}, u32[]{:S(2)}) collective-permute-start(bf16[8,128,2,128]{3,1,2,0:T(8,128)(2,1)S(1)} %collective-permute-done.1), channel_id=1, source_target_pairs={{0,2},{2,4},{4,6},{6,8},{8,10},{10,12},{12,14},{1,3},{3,5},{5,7},{... | collective-permute-start | bytes 1572872 | tf_op jit(solution)/shard_map/ppermute | solution.py:19
  62.9 14.2 %collective-permute-start.3 = (bf16[8,128,2,128]{3,1,2,0:T(8,128)(2,1)S(1)}, bf16[8,128,2,128]{3,1,2,0:T(8,128)(2,1)S(1)}, u32[]{:S(2)}, u32[]{:S(2)}) collective-permute-start(bf16[8,128,2,128]{3,1,2,0:T(8,128)(2,1)S(1)} %collective-permute-done.2), channel_id=1, source_target_pairs={{0,2},{2,4},{4,6},{6,8},{8,10},{10,12},{12,14},{1,3},{3,5},{5,7},{... | collective-permute-start | bytes 1572872 | tf_op jit(solution)/shard_map/ppermute | solution.py:19
  77.1 13.4 %collective-permute-start.4 = (bf16[8,128,2,128]{3,1,2,0:T(8,128)(2,1)S(1)}, bf16[8,128,2,128]{3,1,2,0:T(8,128)(2,1)}, u32[]{:S(2)}, u32[]{:S(2)}) collective-permute-start(bf16[8,128,2,128]{3,1,2,0:T(8,128)(2,1)S(1)} %collective-permute-done.3), channel_id=1, source_target_pairs={{0,2},{2,4},{4,6},{6,8},{8,10},{10,12},{12,14},{1,3},{3,5},{5,7},{... | collective-permute-start | bytes 1572872 | tf_op jit(solution)/shard_map/ppermute | solution.py:19
  90.4 12.8 %collective-permute-start.5 = (bf16[8,128,2,128]{3,1,2,0:T(8,128)(2,1)}, bf16[8,128,2,128]{3,1,2,0:T(8,128)(2,1)}, u32[]{:S(2)}, u32[]{:S(2)}) collective-permute-start(bf16[8,128,2,128]{3,1,2,0:T(8,128)(2,1)} %collective-permute-done.4), channel_id=1, source_target_pairs={{0,2},{2,4},{4,6},{6,8},{8,10},{10,12},{12,14},{1,3},{3,5},{5,7},{... | collective-permute-start | bytes 1572872 | tf_op jit(solution)/shard_map/ppermute | solution.py:19
  105.8 1.8 copy-start
  107.6 7.1 %copy-start.1 = (bf16[8,128,2,128]{3,1,2,0:T(8,128)(2,1)}, bf16[8,128,2,128]{3,1,2,0:T(8,128)(2,1)S(1)}, u32[]{:S(2)}) copy-start(bf16[8,128,2,128]{3,1,2,0:T(8,128)(2,1)S(1)} %get-tuple-element.132) | copy-start | bytes 1572868 | tf_op jit(solution)/shard_map/while
  117.8 3.0 %copy-start.2 = (bf16[8,128,2,128]{3,1,2,0:T(8,128)(2,1)S(1)}, bf16[8,128,2,128]{3,1,2,0:T(8,128)(2,1)}, u32[]{:S(2)}) copy-start(bf16[8,128,2,128]{3,1,2,0:T(8,128)(2,1)} %copy-done.1) | copy-start | bytes 1572868 | tf_op jit(solution)/shard_map/while
  120.9 7.1 %copy-start.1 = (bf16[8,128,2,128]{3,1,2,0:T(8,128)(2,1)}, bf16[8,128,2,128]{3,1,2,0:T(8,128)(2,1)S(1)}, u32[]{:S(2)}) copy-start(bf16[8,128,2,128]{3,1,2,0:T(8,128)(2,1)S(1)} %get-tuple-element.132) | copy-start | bytes 1572868 | tf_op jit(solution)/shard_map/while
  131.1 3.0 %copy-start.2 = (bf16[8,128,2,128]{3,1,2,0:T(8,128)(2,1)S(1)}, bf16[8,128,2,128]{3,1,2,0:T(8,128)(2,1)}, u32[]{:S(2)}) copy-start(bf16[8,128,2,128]{3,1,2,0:T(8,128)(2,1)} %copy-done.1) | copy-start | bytes 1572868 | tf_op jit(solution)/shard_map/while
  134.1 7.1 %copy-start.1 = (bf16[8,128,2,128]{3,1,2,0:T(8,128)(2,1)}, bf16[8,128,2,128]{3,1,2,0:T(8,128)(2,1)S(1)}, u32[]{:S(2)}) copy-start(bf16[8,128,2,128]{3,1,2,0:T(8,128)(2,1)S(1)} %get-tuple-element.132) | copy-start | bytes 1572868 | tf_op jit(solution)/shard_map/while
  144.4 3.0 %copy-start.2 = (bf16[8,128,2,128]{3,1,2,0:T(8,128)(2,1)S(1)}, bf16[8,128,2,128]{3,1,2,0:T(8,128)(2,1)}, u32[]{:S(2)}) copy-start(bf16[8,128,2,128]{3,1,2,0:T(8,128)(2,1)} %copy-done.1) | copy-start | bytes 1572868 | tf_op jit(solution)/shard_map/while
  147.4 7.1 %copy-start.1 = (bf16[8,128,2,128]{3,1,2,0:T(8,128)(2,1)}, bf16[8,128,2,128]{3,1,2,0:T(8,128)(2,1)S(1)}, u32[]{:S(2)}) copy-start(bf16[8,128,2,128]{3,1,2,0:T(8,128)(2,1)S(1)} %get-tuple-element.132) | copy-start | bytes 1572868 | tf_op jit(solution)/shard_map/while
  157.6 3.0 %copy-start.2 = (bf16[8,128,2,128]{3,1,2,0:T(8,128)(2,1)S(1)}, bf16[8,128,2,128]{3,1,2,0:T(8,128)(2,1)}, u32[]{:S(2)}) copy-start(bf16[8,128,2,128]{3,1,2,0:T(8,128)(2,1)} %copy-done.1) | copy-start | bytes 1572868 | tf_op jit(solution)/shard_map/while
  160.7 7.1 %copy-start.1 = (bf16[8,128,2,128]{3,1,2,0:T(8,128)(2,1)}, bf16[8,128,2,128]{3,1,2,0:T(8,128)(2,1)S(1)}, u32[]{:S(2)}) copy-start(bf16[8,128,2,128]{3,1,2,0:T(8,128)(2,1)S(1)} %get-tuple-element.132) | copy-start | bytes 1572868 | tf_op jit(solution)/shard_map/while
  170.9 3.0 %copy-start.2 = (bf16[8,128,2,128]{3,1,2,0:T(8,128)(2,1)S(1)}, bf16[8,128,2,128]{3,1,2,0:T(8,128)(2,1)}, u32[]{:S(2)}) copy-start(bf16[8,128,2,128]{3,1,2,0:T(8,128)(2,1)} %copy-done.1) | copy-start | bytes 1572868 | tf_op jit(solution)/shard_map/while
  174.0 7.1 %copy-start.1 = (bf16[8,128,2,128]{3,1,2,0:T(8,128)(2,1)}, bf16[8,128,2,128]{3,1,2,0:T(8,128)(2,1)S(1)}, u32[]{:S(2)}) copy-start(bf16[8,128,2,128]{3,1,2,0:T(8,128)(2,1)S(1)} %get-tuple-element.132) | copy-start | bytes 1572868 | tf_op jit(solution)/shard_map/while
  184.2 3.0 %copy-start.2 = (bf16[8,128,2,128]{3,1,2,0:T(8,128)(2,1)S(1)}, bf16[8,128,2,128]{3,1,2,0:T(8,128)(2,1)}, u32[]{:S(2)}) copy-start(bf16[8,128,2,128]{3,1,2,0:T(8,128)(2,1)} %copy-done.1) | copy-start | bytes 1572868 | tf_op jit(solution)/shard_map/while
  187.2 7.1 %copy-start.1 = (bf16[8,128,2,128]{3,1,2,0:T(8,128)(2,1)}, bf16[8,128,2,128]{3,1,2,0:T(8,128)(2,1)S(1)}, u32[]{:S(2)}) copy-start(bf16[8,128,2,128]{3,1,2,0:T(8,128)(2,1)S(1)} %get-tuple-element.132) | copy-start | bytes 1572868 | tf_op jit(solution)/shard_map/while
  197.5 3.0 %copy-start.2 = (bf16[8,128,2,128]{3,1,2,0:T(8,128)(2,1)S(1)}, bf16[8,128,2,128]{3,1,2,0:T(8,128)(2,1)}, u32[]{:S(2)}) copy-start(bf16[8,128,2,128]{3,1,2,0:T(8,128)(2,1)} %copy-done.1) | copy-start | bytes 1572868 | tf_op jit(solution)/shard_map/while
  200.5 7.1 %copy-start.1 = (bf16[8,128,2,128]{3,1,2,0:T(8,128)(2,1)}, bf16[8,128,2,128]{3,1,2,0:T(8,128)(2,1)S(1)}, u32[]{:S(2)}) copy-start(bf16[8,128,2,128]{3,1,2,0:T(8,128)(2,1)S(1)} %get-tuple-element.132) | copy-start | bytes 1572868 | tf_op jit(solution)/shard_map/while
  210.7 3.0 %copy-start.2 = (bf16[8,128,2,128]{3,1,2,0:T(8,128)(2,1)S(1)}, bf16[8,128,2,128]{3,1,2,0:T(8,128)(2,1)}, u32[]{:S(2)}) copy-start(bf16[8,128,2,128]{3,1,2,0:T(8,128)(2,1)} %copy-done.1) | copy-start | bytes 1572868 | tf_op jit(solution)/shard_map/while
  213.8 0.6 copy-start.3
Sparse Core Ops, SparseCore 0:
  214.6 11.6 reduce-scatter.1
where the time goes:
time: 236 us; the launch traced here: 235 us
  waiting for transfers between devices  66.3 us (28%)
  local copies, waits for them, and re-layouts  35.3 us (15%)
  other arithmetic  35 us (15%)
  starting transfers between devices  31 us (13%)
  matrix products  25.6 us (11%)
  loops' own time  25.3 us (11%)
  between operations  13.5 us (6%)
  blocking collectives  2.63 us (1%)
    ppermute x6, waiting for transfers between devices, shifted(): lax.ppermute(value, axis, [(source, source + steps) for source in range(i...  54.4 us
    ppermute x6, starting transfers between devices, shifted(): lax.ppermute(value, axis, [(source, source + steps) for source in range(i...  31 us
    another operation x10, other arithmetic  26.8 us
    another operation x1, loops' own time, shards(): lax.map(one_window, jnp.arange(lax.axis_size('chan') * (windows // chan_c...  25.3 us
    dot_general x8, matrix products, window_terms(): lagged = jnp.dot(flattened, lag_rows, preferred_element_type=jnp.float32)  23.9 us
    another operation x8, local copies, waits for them, and re-layouts, window_terms(): cross_spec = jnp.stack([prod_real, prod_imag], axis=2).astype(jnp.bfloat16)  22.6 us
    reduce_scatter x1, waiting for transfers between devices, shards(): lax.psum_scatter(lax.map(one_window, jnp.arange(lax.axis_size('chan') * (...  11.9 us
    dynamic_slice x8, local copies, waits for them, and re-layouts, shards(): lax.map(one_window, jnp.arange(lax.axis_size('chan') * (windows // chan_c...  5.37 us
  transfers between devices with their start and end apart: 7, of which 7 were waited for; matrix products, arithmetic and copies ran while one was open for 0% of the time, Pallas kernels for 0%

commit v1 on v0

--- a/solution.py
+++ b/solution.py
@@ -1,8 +1,11 @@
+import functools
 import math
 
 import jax
 import jax.numpy as jnp
 from jax import lax
+from jax.experimental import pallas as pl
+from jax.experimental.pallas import tpu as pltpu
 from jax.sharding import PartitionSpec as P
 
 LAGS = 128
@@ -60,7 +63,7 @@
     return jnp.sum(lagged * lagged, axis=1)
 
 
-def shards(spectra, offsets, channel_group):
+def ring_shards(spectra, offsets, channel_group):
     windows = spectra.shape[0]
     local_chans = spectra.shape[1]
     freq_bins = spectra.shape[3]
@@ -99,6 +102,288 @@
     ).astype(jnp.float32)
 
 
+HIGHEST = lax.Precision.HIGHEST
+
+
+def phase_of(turns, freq_bins):
+    period = 2.0 * freq_bins
+    return (jnp.pi / freq_bins) * (turns - period * jnp.floor(turns / period))
+
+
+def kernel(
+    n, chans, windows, share, freq_bins, cores,
+    x_ref, off_ref, group_ref, out_ref,
+    local, wide, raw, unpacked, tile, tiles, table, aligned, part, half_out, half_in, sum_out, sum_in,
+    local_sem, keep_sem, x_send, x_recv, e_send, e_recv, h_send, h_recv, s_send, s_recv,
+):
+    me = lax.axis_index("tm")
+    core = lax.axis_index("chan")
+    total = n * windows
+    band = SPAN * windows
+    block = 2 * windows
+    blocks = band // block
+    pad = block
+    mine = windows // cores
+    lanes = freq_bins
+
+    load = pltpu.make_async_copy(x_ref, local, local_sem)
+    load.start()
+    keep = pltpu.make_async_copy(x_ref.at[:, pl.ds(me * 2 * share, 2 * share), :], raw.at[me], keep_sem)
+    keep.start()
+
+    barrier = pltpu.get_barrier_semaphore()
+    for d in range(n):
+        for k in range(cores):
+            if d or k:
+                pl.semaphore_signal(
+                    barrier, inc=1,
+                    device_id={"tm": lax.rem(me + d, n), "chan": lax.rem(core + k, cores)},
+                    device_id_type=pl.DeviceIdType.MESH,
+                )
+    pl.semaphore_wait(barrier, n * cores - 1)
+
+    def x_copy(there, slot):
+        return pltpu.make_async_remote_copy(
+            src_ref=x_ref.at[:, pl.ds(there * 2 * share, 2 * share), :],
+            dst_ref=raw.at[slot],
+            send_sem=x_send.at[there],
+            recv_sem=x_recv.at[slot],
+            device_id={"tm": there},
+            device_id_type=pl.DeviceIdType.MESH,
+        )
+
+    for d in range(1, n):
+        x_copy(lax.rem(me + d, n), me).start()
+
+    load.wait()
+    for w in range(windows):
+        wide[pl.ds(w * 2 * chans, 2 * chans), :] = local[w].astype(jnp.float32)
+    lane = lax.broadcasted_iota(jnp.int32, (windows, lanes), 1)
+    row = lax.broadcasted_iota(jnp.int32, (windows, lanes), 0)
+
+    def power_step(c, held):
+        real = wide[pl.ds(2 * c, windows, stride=2 * chans), :]
+        imag = wide[pl.ds(2 * c + 1, windows, stride=2 * chans), :]
+        power = jnp.sum(real * real + imag * imag, axis=1, keepdims=True)
+        return jnp.where(lane == c, power, held)
+
+    chan_power = lax.fori_loop(0, chans, power_step, jnp.zeros((windows, lanes), jnp.float32), unroll=8)
+    group_id = lax.broadcasted_iota(jnp.int32, (lanes, chans), 0)
+    onehot = (group_id == group_ref[...]).astype(jnp.float32)
+    totals = lax.dot_general(
+        chan_power, onehot, (((1,), (1,)), ((), ())), precision=HIGHEST, preferred_element_type=jnp.float32
+    )
+    for w in range(windows):
+        totals = jnp.where((lane == lanes - 1) & (row == w), off_ref[w].astype(jnp.float32), totals)
+    tile[...] = totals
+
+    def e_copy(there, other, slot):
+        return pltpu.make_async_remote_copy(
+            src_ref=tile,
+            dst_ref=tiles.at[slot],
+            send_sem=e_send.at[there * cores + other],
+            recv_sem=e_recv.at[slot],
+            device_id={"tm": there, "chan": other},
+            device_id_type=pl.DeviceIdType.MESH,
+        )
+
+    def others():
+        for d in range(n):
+            for k in range(cores):
+                if d or k:
+                    yield lax.rem(me + d, n), lax.rem(core + k, cores)
+
+    for there, other in others():
+        e_copy(there, other, me * cores + core).start()
+    tiles[me * cores + core] = totals
+
+    frequency = lax.broadcasted_iota(jnp.int32, (freq_bins, LAGS), 0)
+    shift = lax.broadcasted_iota(jnp.int32, (freq_bins, LAGS), 1) - LAGS // 2
+    angle = phase_of((frequency * shift).astype(jnp.float32), freq_bins)
+    normaliser = 1.0 / math.sqrt(freq_bins)
+    table[pl.ds(0, freq_bins), :] = (jnp.cos(angle) * normaliser).astype(jnp.bfloat16)
+    table[pl.ds(freq_bins, freq_bins), :] = (-jnp.sin(angle) * normaliser).astype(jnp.bfloat16)
+    aligned[:, :, pl.ds(0, pad), :] = jnp.zeros((share, 2, pad, freq_bins), jnp.float32)
+    part[...] = jnp.zeros_like(part)
+
+    my_onehot = (group_id == pltpu.roll(group_ref[...], lax.rem(chans - me * share, chans), 1)).astype(jnp.float32)
+    bins = lax.broadcasted_iota(jnp.int32, (windows, freq_bins), 1).astype(jnp.float32)
+    keep.wait()
+    for there, other in others():
+        e_copy(there, other, there * cores + other).wait_recv()
+
+    def align_step(i, carry):
+        t = lax.rem(me + n - i, n)
+
+        @pl.when(i > 0)
+        def _():
+            x_copy(t, t).wait_recv()
+
+        for w in range(windows):
+            unpacked[pl.ds(w * 2 * share, 2 * share), :] = raw[t, w].astype(jnp.float32)
+        first = tiles[t * cores]
+        summed = first
+        for k in range(1, cores):
+            summed = summed + tiles[t * cores + k]
+        energy = summed * (GROUPS / (freq_bins * chans * cores))
+        scales = jnp.dot(
+            lax.rsqrt(energy + epsilon), my_onehot, precision=HIGHEST, preferred_element_type=jnp.float32
+        )
+        theta = phase_of(bins * first[:, lanes - 1 : lanes], freq_bins)
+        cosine = jnp.cos(theta)
+        sine = jnp.sin(theta)
+        for c in range(share):
+            real = unpacked[pl.ds(2 * c, windows, stride=2 * share), :]
+            imag = unpacked[pl.ds(2 * c + 1, windows, stride=2 * share), :]
+            weight = scales[:, c : c + 1]
+            out_real = weight * (real * cosine + imag * sine)
+            out_imag = weight * (imag * cosine - real * sine)
+            place = pl.ds(pl.multiple_of(pad + t * windows, windows), windows)
+            aligned[c, 0, place, :] = out_real.astype(jnp.bfloat16).astype(jnp.float32)
+            aligned[c, 1, place, :] = out_imag.astype(jnp.bfloat16).astype(jnp.float32)
+        return carry
+
+    lax.fori_loop(0, n, align_step, 0)
+
+    def pair_block(w, k):
+        start = pad + w - band + k * block
+        rows = []
+        for c in range(share):
+            left_real = aligned[c, 0, pl.ds(pad + w, 1), :]
+            left_imag = aligned[c, 1, pl.ds(pad + w, 1), :]
+            right_real = aligned[c, 0, pl.ds(start, block), :]
+            right_imag = aligned[c, 1, pl.ds(start, block), :]
+            prod_real = left_real * right_real + left_imag * right_imag
+            prod_imag = left_imag * right_real - left_real * right_imag
+            rows.append(
+                jnp.concatenate([prod_real.astype(jnp.bfloat16), prod_imag.astype(jnp.bfloat16)], axis=1)
+            )
+        lagged = jnp.dot(jnp.concatenate(rows, axis=0), table[...], preferred_element_type=jnp.float32)
+        lagged = lagged.reshape(share, block, LAGS)
+        part[w, pl.ds(pl.multiple_of(k * block, block), block), :] = jnp.sum(lagged * lagged, axis=0)
+
+    def h_copy(t):
+        return pltpu.make_async_remote_copy(
+            src_ref=half_out.at[t],
+            dst_ref=half_in.at[t],
+            send_sem=h_send.at[t],
+            recv_sem=h_recv.at[t],
+            device_id={"chan": 1 - core},
+            device_id_type=pl.DeviceIdType.MESH,
+        )
+
+    def s_copy(t, slot):
+        return pltpu.make_async_remote_copy(
+            src_ref=sum_out.at[t],
+            dst_ref=sum_in.at[slot],
+            send_sem=s_send.at[t],
+            recv_sem=s_recv.at[slot],
+            device_id={"tm": t},
+            device_id_type=pl.DeviceIdType.MESH,
+        )
+
+    def pass_on(t):
+        h_copy(t).wait_recv()
+        return part[pl.ds(t * windows + core * mine, mine)] + half_in[t].astype(jnp.float32)
+
+    def stage(i, carry):
+        t = lax.rem(me + 1 + i, n)
+
+        def one_window(j, held):
+            w = t * windows + j
+            first = jnp.maximum(band - w, 0) // block
+
+            def one_block(k, inner):
+                pair_block(w, k)
+                return inner
+
+            lax.fori_loop(first, blocks, one_block, 0)
+            return held
+
+        lax.fori_loop(0, windows, one_window, 0)
+        half_out[t] = part[pl.ds(t * windows + (1 - core) * mine, mine)].astype(jnp.bfloat16)
+        h_copy(t).start()
+
+        @pl.when(i > 0)
+        def _():
+            before = lax.rem(me + i, n)
+            sum_out[before] = pass_on(before).astype(jnp.bfloat16)
+            s_copy(before, me).start()
+
+        return carry
+
+    lax.fori_loop(0, n, stage, 0)
+    result = pass_on(me)
+    for d in range(1, n):
+        s = lax.rem(me + n - d, n)
+        s_copy(s, s).wait_recv()
+        result = result + sum_in[s].astype(jnp.float32)
+    out_ref[...] = result * (1.0 / (chans * cores))
+
+    for d in range(1, n):
+        t = lax.rem(me + d, n)
+        x_copy(t, me).wait_send()
+        s_copy(t, me).wait_send()
+    for t in range(n):
+        h_copy(t).wait_send()
+    for there, other in others():
+        e_copy(there, other, me * cores + core).wait_send()
+
+
+def spread_shards(spectra, offsets, channel_group):
+    windows, chans, _, freq_bins = spectra.shape
+    n = lax.axis_size("tm")
+    cores = lax.axis_size("chan")
+    share = chans // n
+    total = n * windows
+    band = SPAN * windows
+    mine = windows // cores
+    dma = pltpu.SemaphoreType.DMA
+    return pl.pallas_call(
+        functools.partial(kernel, n, chans, windows, share, freq_bins, cores),
+        out_shape=jax.ShapeDtypeStruct((mine, band, LAGS), jnp.float32),
+        in_specs=[
+            pl.BlockSpec(memory_space=pl.ANY),
+            pl.BlockSpec(memory_space=pltpu.SMEM),
+            pl.BlockSpec(memory_space=pltpu.VMEM),
+        ],
+        out_specs=pl.BlockSpec(memory_space=pltpu.VMEM),
+        scratch_shapes=[
+            pltpu.VMEM((windows, 2 * chans, freq_bins), jnp.bfloat16),
+            pltpu.VMEM((windows * 2 * chans, freq_bins), jnp.float32),
+            pltpu.VMEM((n, windows, 2 * share, freq_bins), jnp.bfloat16),
+            pltpu.VMEM((windows * 2 * share, freq_bins), jnp.float32),
+            pltpu.VMEM((windows, freq_bins), jnp.float32),
+            pltpu.VMEM((n * cores, windows, freq_bins), jnp.float32),
+            pltpu.VMEM((2 * freq_bins, LAGS), jnp.bfloat16),
+            pltpu.VMEM((share, 2, total + 2 * windows, freq_bins), jnp.float32),
+            pltpu.VMEM((total, band, LAGS), jnp.float32),
+            pltpu.VMEM((n, mine, band, LAGS), jnp.bfloat16),
+            pltpu.VMEM((n, mine, band, LAGS), jnp.bfloat16),
+            pltpu.VMEM((n, mine, band, LAGS), jnp.bfloat16),
+            pltpu.VMEM((n, mine, band, LAGS), jnp.bfloat16),
+            dma, dma, dma((n,)), dma((n,)), dma((n * cores,)), dma((n * cores,)),
+            dma((n,)), dma((n,)), dma((n,)), dma((n,)),
+        ],
+        compiler_params=pltpu.CompilerParams(
+            collective_id=0, has_side_effects=True, vmem_limit_bytes=56 * 1024 * 1024
+        ),
+    )(spectra.reshape(windows, 2 * chans, freq_bins), offsets, channel_group.reshape(1, chans))
+
+
+def shards(spectra, offsets, channel_group):
+    windows, chans, _, freq_bins = spectra.shape
+    n = lax.axis_size("tm")
+    fits = (
+        chans == freq_bins == LAGS == 128
+        and windows == 8
+        and lax.axis_size("chan") == 2
+        and chans % n == 0
+        and chans // n >= 8
+    )
+    return (spread_shards if fits else ring_shards)(spectra, offsets, channel_group)
+
+
 def solution(mesh):
     placed = (P(("arrays", "tm"), "chan", None, None), P(("arrays", "tm")), P(("arrays", "chan")))
     return jax.shard_map(

time: 236 us -> 56.9 us (0.24)
  waiting for transfers between devices: 66.3 us -> 0 us
  Pallas kernels: 0 us -> 55.2 us
  other arithmetic: 35 us -> 0 us
  local copies, waits for them, and re-layouts: 35.3 us -> 1.54 us
  starting transfers between devices: 31 us -> 0 us
  matrix products: 25.6 us -> 0 us
  loops' own time: 25.3 us -> 0 us
  between operations: 13.5 us -> 0.01 us
  blocking collectives: 2.63 us -> 0 us
    pallas_call x0 -> x1, Pallas kernels: none -> 55.2 us  [spread_shards(): pl.pallas_call(functools.partial(kernel, n, chans, windows, share, freq_b...]
    ppermute x6 -> x0, waiting for transfers between devices: 54.4 us -> none  [shifted(): lax.ppermute(value, axis, [(source, source + steps) for source in range(i...]
    ppermute x6 -> x0, starting transfers between devices: 31 us -> none  [shifted(): lax.ppermute(value, axis, [(source, source + steps) for source in range(i...]
    another operation x19 -> x0, other arithmetic: 29.3 us -> none
    dot_general x10 -> x0, matrix products: 25.6 us -> none  [the longest x8 23.9 us: window_terms(): lagged = jnp.dot(flattened, lag_rows, preferred_element_type=jnp.float32)]
    another operation x1 -> x0, loops' own time: 25.3 us -> none  [shards(): lax.map(one_window, jnp.arange(lax.axis_size('chan') * (windows // chan_c...]
    another operation x8 -> x0, local copies, waits for them, and re-layouts: 22.6 us -> none  [window_terms(): cross_spec = jnp.stack([prod_real, prod_imag], axis=2).astype(jnp.bfloat16)]
    reduce_scatter x1 -> x0, waiting for transfers between devices: 11.9 us -> none  [shards(): lax.psum_scatter(lax.map(one_window, jnp.arange(lax.axis_size('chan') * (...]
  transfers between devices with their start and end apart: 7 -> 0, of which waited for: 7 -> 0; matrix products, arithmetic and copies ran while one was open for 0% -> 0% of each run, Pallas kernels for 0% -> 0%
where the time goes in v1:
time: 56.9 us; the launch traced here: 56.8 us
  Pallas kernels  55.2 us (97%)
  local copies, waits for them, and re-layouts  1.54 us (3%)
    pallas_call x1, Pallas kernels, spread_shards(): pl.pallas_call(functools.partial(kernel, n, chans, windows, share, freq_b...  55.2 us
    unnamed x1, local copies, waits for them, and re-layouts  1.54 us

profile of v1, /device:TPU:0, one launch (start us, length us, event | category | flops | bytes accessed | tf_op | source)
XLA Modules:
  0.0 56.8 jit_solution(3848120575174187067)
XLA Ops:
  0.0 55.2 %shard_map.37 = f32[4,48,128]{2,1,0:T(8,128)} custom-call(bf16[8,256,128]{2,1,0:T(8,128)(2,1)} %bitcast.2, s32[8]{0:T(128)} %off_ref.1, s32[1,128]{1,0:T(1,128)} %bitcast.3), custom_call_target="tpu_custom_call" | custom-call | tf_op jit(solution)/shard_map/pallas_call | solution.py:342
  55.2 1.5 %copy.5 = f32[4,48,128]{2,1,0:T(8,128)} copy(f32[4,48,128]{2,1,0:T(8,128)} %shard_map.37) | data formatting | bytes 196608

commit v2 on v1

--- a/solution.py
+++ b/solution.py
@@ -113,16 +113,12 @@
 def kernel(
     n, chans, windows, share, freq_bins, cores,
     x_ref, off_ref, group_ref, out_ref,
-    local, wide, raw, unpacked, tile, tiles, table, aligned, part, half_out, half_in, sum_out, sum_in,
+    local, wide, raw, unpacked, tile, tiles, table, right, left, part, half_out, half_in, sum_out, sum_in,
     local_sem, keep_sem, x_send, x_recv, e_send, e_recv, h_send, h_recv, s_send, s_recv,
 ):
     me = lax.axis_index("tm")
     core = lax.axis_index("chan")
-    total = n * windows
     band = SPAN * windows
-    block = 2 * windows
-    blocks = band // block
-    pad = block
     mine = windows // cores
     lanes = freq_bins
 
@@ -203,7 +199,6 @@
     normaliser = 1.0 / math.sqrt(freq_bins)
     table[pl.ds(0, freq_bins), :] = (jnp.cos(angle) * normaliser).astype(jnp.bfloat16)
     table[pl.ds(freq_bins, freq_bins), :] = (-jnp.sin(angle) * normaliser).astype(jnp.bfloat16)
-    aligned[:, :, pl.ds(0, pad), :] = jnp.zeros((share, 2, pad, freq_bins), jnp.float32)
     part[...] = jnp.zeros_like(part)
 
     my_onehot = (group_id == pltpu.roll(group_ref[...], lax.rem(chans - me * share, chans), 1)).astype(jnp.float32)
@@ -232,35 +227,37 @@
         theta = phase_of(bins * first[:, lanes - 1 : lanes], freq_bins)
         cosine = jnp.cos(theta)
         sine = jnp.sin(theta)
-        for c in range(share):
-            real = unpacked[pl.ds(2 * c, windows, stride=2 * share), :]
-            imag = unpacked[pl.ds(2 * c + 1, windows, stride=2 * share), :]
-            weight = scales[:, c : c + 1]
-            out_real = weight * (real * cosine + imag * sine)
-            out_imag = weight * (imag * cosine - real * sine)
-            place = pl.ds(pl.multiple_of(pad + t * windows, windows), windows)
-            aligned[c, 0, place, :] = out_real.astype(jnp.bfloat16).astype(jnp.float32)
-            aligned[c, 1, place, :] = out_imag.astype(jnp.bfloat16).astype(jnp.float32)
+        for p in range(share // 2):
+            pair = []
+            for c in (2 * p, 2 * p + 1):
+                real = unpacked[pl.ds(2 * c, windows, stride=2 * share), :]
+                imag = unpacked[pl.ds(2 * c + 1, windows, stride=2 * share), :]
+                weight = scales[:, c : c + 1]
+                pair.append((weight * (real * cosine + imag * sine), weight * (imag * cosine - real * sine)))
+            for r in range(2):
+                right[p, r, t] = jnp.concatenate([pair[0][r], pair[1][r]], axis=0).astype(jnp.bfloat16)
+                for j in range(windows):
+                    spread = [jnp.broadcast_to(x[r][j : j + 1, :], (windows, freq_bins)) for x in pair]
+                    left[t * windows + j, p, r] = jnp.concatenate(spread, axis=0).astype(jnp.bfloat16)
         return carry
 
     lax.fori_loop(0, n, align_step, 0)
 
-    def pair_block(w, k):
-        start = pad + w - band + k * block
-        rows = []
-        for c in range(share):
-            left_real = aligned[c, 0, pl.ds(pad + w, 1), :]
-            left_imag = aligned[c, 1, pl.ds(pad + w, 1), :]
-            right_real = aligned[c, 0, pl.ds(start, block), :]
-            right_imag = aligned[c, 1, pl.ds(start, block), :]
-            prod_real = left_real * right_real + left_imag * right_imag
-            prod_imag = left_imag * right_real - left_real * right_imag
-            rows.append(
-                jnp.concatenate([prod_real.astype(jnp.bfloat16), prod_imag.astype(jnp.bfloat16)], axis=1)
-            )
-        lagged = jnp.dot(jnp.concatenate(rows, axis=0), table[...], preferred_element_type=jnp.float32)
-        lagged = lagged.reshape(share, block, LAGS)
-        part[w, pl.ds(pl.multiple_of(k * block, block), block), :] = jnp.sum(lagged * lagged, axis=0)
+    def pair_block(t, s):
+        rights = [(right[p, 0, s], right[p, 1, s]) for p in range(share // 2)]
+        for j in range(windows):
+            w = t * windows + j
+            rows = []
+            for p, (right_real, right_imag) in enumerate(rights):
+                left_real = left[w, p, 0]
+                left_imag = left[w, p, 1]
+                prod_real = left_real * right_real + left_imag * right_imag
+                prod_imag = left_imag * right_real - left_real * right_imag
+                rows.append(jnp.concatenate([prod_real, prod_imag], axis=1))
+            lagged = jnp.dot(jnp.concatenate(rows, axis=0), table[...], preferred_element_type=jnp.float32)
+            lagged = lagged.reshape(share, windows, LAGS)
+            place = band + windows + s * windows - w
+            part[w, pl.ds(place, windows), :] = jnp.sum(lagged * lagged, axis=0)
 
     def h_copy(t):
         return pltpu.make_async_remote_copy(
@@ -284,24 +281,17 @@
 
     def pass_on(t):
         h_copy(t).wait_recv()
-        return part[pl.ds(t * windows + core * mine, mine)] + half_in[t].astype(jnp.float32)
+        return part[pl.ds(t * windows + core * mine, mine), pl.ds(windows, band), :] + half_in[t].astype(jnp.float32)
 
     def stage(i, carry):
         t = lax.rem(me + 1 + i, n)
 
-        def one_window(j, held):
-            w = t * windows + j
-            first = jnp.maximum(band - w, 0) // block
-
-            def one_block(k, inner):
-                pair_block(w, k)
-                return inner
-
-            lax.fori_loop(first, blocks, one_block, 0)
+        def one_block(s, held):
+            pair_block(t, s)
             return held
 
-        lax.fori_loop(0, windows, one_window, 0)
-        half_out[t] = part[pl.ds(t * windows + (1 - core) * mine, mine)].astype(jnp.bfloat16)
+        lax.fori_loop(jnp.maximum(t - SPAN, 0), t + 1, one_block, 0)
+        half_out[t] = part[pl.ds(t * windows + (1 - core) * mine, mine), pl.ds(windows, band), :].astype(jnp.bfloat16)
         h_copy(t).start()
 
         @pl.when(i > 0)
@@ -356,8 +346,9 @@
             pltpu.VMEM((windows, freq_bins), jnp.float32),
             pltpu.VMEM((n * cores, windows, freq_bins), jnp.float32),
             pltpu.VMEM((2 * freq_bins, LAGS), jnp.bfloat16),
-            pltpu.VMEM((share, 2, total + 2 * windows, freq_bins), jnp.float32),
-            pltpu.VMEM((total, band, LAGS), jnp.float32),
+            pltpu.VMEM((share // 2, 2, n, 2 * windows, freq_bins), jnp.bfloat16),
+            pltpu.VMEM((total, share // 2, 2, 2 * windows, freq_bins), jnp.bfloat16),
+            pltpu.VMEM((total, band + 2 * windows, LAGS), jnp.float32),
             pltpu.VMEM((n, mine, band, LAGS), jnp.bfloat16),
             pltpu.VMEM((n, mine, band, LAGS), jnp.bfloat16),
             pltpu.VMEM((n, mine, band, LAGS), jnp.bfloat16),

time: 56.9 us -> 41.9 us (0.74)
  Pallas kernels: 55.2 us -> 40.2 us
    pallas_call x1, Pallas kernels: 55.2 us -> 40.2 us  [spread_shards(): pl.pallas_call(functools.partial(kernel, n, chans, windows, share, freq_b...]
where the time goes in v2:
time: 41.9 us; the launch traced here: 41.8 us
  Pallas kernels  40.2 us (96%)
  local copies, waits for them, and re-layouts  1.54 us (4%)
    pallas_call x1, Pallas kernels, spread_shards(): pl.pallas_call(functools.partial(kernel, n, chans, windows, share, freq_b...  40.2 us
    unnamed x1, local copies, waits for them, and re-layouts  1.54 us

profile of v2, /device:TPU:0, one launch (start us, length us, event | category | flops | bytes accessed | tf_op | source)
XLA Modules:
  0.0 41.8 jit_solution(18274568737464410880)
XLA Ops:
  0.0 40.2 %shard_map.37 = f32[4,48,128]{2,1,0:T(8,128)} custom-call(bf16[8,256,128]{2,1,0:T(8,128)(2,1)} %bitcast.2, s32[8]{0:T(128)} %off_ref.1, s32[1,128]{1,0:T(1,128)} %bitcast.3), custom_call_target="tpu_custom_call" | custom-call | tf_op jit(solution)/shard_map/pallas_call | solution.py:332
  40.2 1.5 %copy.5 = f32[4,48,128]{2,1,0:T(8,128)} copy(f32[4,48,128]{2,1,0:T(8,128)} %shard_map.37) | data formatting | bytes 196608

commit v3 on v2

--- a/solution.py
+++ b/solution.py
@@ -136,8 +136,6 @@
                     device_id={"tm": lax.rem(me + d, n), "chan": lax.rem(core + k, cores)},
                     device_id_type=pl.DeviceIdType.MESH,
                 )
-    pl.semaphore_wait(barrier, n * cores - 1)
-
     def x_copy(there, slot):
         return pltpu.make_async_remote_copy(
             src_ref=x_ref.at[:, pl.ds(there * 2 * share, 2 * share), :],
@@ -148,9 +146,6 @@
             device_id_type=pl.DeviceIdType.MESH,
         )
 
-    for d in range(1, n):
-        x_copy(lax.rem(me + d, n), me).start()
-
     load.wait()
     for w in range(windows):
         wide[pl.ds(w * 2 * chans, 2 * chans), :] = local[w].astype(jnp.float32)
@@ -189,8 +184,11 @@
                 if d or k:
                     yield lax.rem(me + d, n), lax.rem(core + k, cores)
 
+    pl.semaphore_wait(barrier, n * cores - 1)
     for there, other in others():
         e_copy(there, other, me * cores + core).start()
+    for d in range(1, n):
+        x_copy(lax.rem(me + d, n), me).start()
     tiles[me * cores + core] = totals
 
     frequency = lax.broadcasted_iota(jnp.int32, (freq_bins, LAGS), 0)
@@ -227,33 +225,28 @@
         theta = phase_of(bins * first[:, lanes - 1 : lanes], freq_bins)
         cosine = jnp.cos(theta)
         sine = jnp.sin(theta)
-        for p in range(share // 2):
-            pair = []
-            for c in (2 * p, 2 * p + 1):
-                real = unpacked[pl.ds(2 * c, windows, stride=2 * share), :]
-                imag = unpacked[pl.ds(2 * c + 1, windows, stride=2 * share), :]
-                weight = scales[:, c : c + 1]
-                pair.append((weight * (real * cosine + imag * sine), weight * (imag * cosine - real * sine)))
-            for r in range(2):
-                right[p, r, t] = jnp.concatenate([pair[0][r], pair[1][r]], axis=0).astype(jnp.bfloat16)
-                for j in range(windows):
-                    spread = [jnp.broadcast_to(x[r][j : j + 1, :], (windows, freq_bins)) for x in pair]
-                    left[t * windows + j, p, r] = jnp.concatenate(spread, axis=0).astype(jnp.bfloat16)
+        for c in range(share):
+            real = unpacked[pl.ds(2 * c, windows, stride=2 * share), :]
+            imag = unpacked[pl.ds(2 * c + 1, windows, stride=2 * share), :]
+            weight = scales[:, c : c + 1]
+            out_real = weight * (real * cosine + imag * sine)
+            out_imag = weight * (imag * cosine - real * sine)
+            right[c, 0, t] = jnp.concatenate([out_real, out_imag], axis=1).astype(jnp.bfloat16)
+            right[c, 1, t] = jnp.concatenate([out_imag, out_real], axis=1).astype(jnp.bfloat16)
+            for j in range(windows):
+                one_real = jnp.broadcast_to(out_real[j : j + 1, :], (windows, freq_bins))
+                one_imag = jnp.broadcast_to(out_imag[j : j + 1, :], (windows, freq_bins))
+                w = t * windows + j
+                left[w, c, 0] = jnp.concatenate([one_real, -one_real], axis=1).astype(jnp.bfloat16)
+                left[w, c, 1] = jnp.concatenate([one_imag, one_imag], axis=1).astype(jnp.bfloat16)
         return carry
 
     lax.fori_loop(0, n, align_step, 0)
 
     def pair_block(t, s):
-        rights = [(right[p, 0, s], right[p, 1, s]) for p in range(share // 2)]
         for j in range(windows):
             w = t * windows + j
-            rows = []
-            for p, (right_real, right_imag) in enumerate(rights):
-                left_real = left[w, p, 0]
-                left_imag = left[w, p, 1]
-                prod_real = left_real * right_real + left_imag * right_imag
-                prod_imag = left_imag * right_real - left_real * right_imag
-                rows.append(jnp.concatenate([prod_real, prod_imag], axis=1))
+            rows = [left[w, c, 0] * right[c, 0, s] + left[w, c, 1] * right[c, 1, s] for c in range(share)]
             lagged = jnp.dot(jnp.concatenate(rows, axis=0), table[...], preferred_element_type=jnp.float32)
             lagged = lagged.reshape(share, windows, LAGS)
             place = band + windows + s * windows - w
@@ -346,8 +339,8 @@
             pltpu.VMEM((windows, freq_bins), jnp.float32),
             pltpu.VMEM((n * cores, windows, freq_bins), jnp.float32),
             pltpu.VMEM((2 * freq_bins, LAGS), jnp.bfloat16),
-            pltpu.VMEM((share // 2, 2, n, 2 * windows, freq_bins), jnp.bfloat16),
-            pltpu.VMEM((total, share // 2, 2, 2 * windows, freq_bins), jnp.bfloat16),
+            pltpu.VMEM((share, 2, n, windows, 2 * freq_bins), jnp.bfloat16),
+            pltpu.VMEM((total, share, 2, windows, 2 * freq_bins), jnp.bfloat16),
             pltpu.VMEM((total, band + 2 * windows, LAGS), jnp.float32),
             pltpu.VMEM((n, mine, band, LAGS), jnp.bfloat16),
             pltpu.VMEM((n, mine, band, LAGS), jnp.bfloat16),

time: 41.9 us -> 39.7 us (0.947)
  Pallas kernels: 40.2 us -> 38 us
    pallas_call x1, Pallas kernels: 40.2 us -> 38 us  [spread_shards(): pl.pallas_call(functools.partial(kernel, n, chans, windows, share, freq_b...]
where the time goes in v3:
time: 39.7 us; the launch traced here: 39.6 us
  Pallas kernels  38 us (96%)
  local copies, waits for them, and re-layouts  1.54 us (4%)
    pallas_call x1, Pallas kernels, spread_shards(): pl.pallas_call(functools.partial(kernel, n, chans, windows, share, freq_b...  38 us
    unnamed x1, local copies, waits for them, and re-layouts  1.54 us

profile of v3, /device:TPU:0, one launch (start us, length us, event | category | flops | bytes accessed | tf_op | source)
XLA Modules:
  0.0 39.6 jit_solution(979725324306338899)
XLA Ops:
  0.0 38.0 %shard_map.37 = f32[4,48,128]{2,1,0:T(8,128)} custom-call(bf16[8,256,128]{2,1,0:T(8,128)(2,1)} %bitcast.2, s32[8]{0:T(128)} %off_ref.1, s32[1,128]{1,0:T(1,128)} %bitcast.3), custom_call_target="tpu_custom_call" | custom-call | tf_op jit(solution)/shard_map/pallas_call | solution.py:325
  38.0 1.5 %copy.5 = f32[4,48,128]{2,1,0:T(8,128)} copy(f32[4,48,128]{2,1,0:T(8,128)} %shard_map.37) | data formatting | bytes 196608

commit v4 on v3

--- a/solution.py
+++ b/solution.py
@@ -102,6 +102,7 @@
     ).astype(jnp.float32)
 
 
+LATE = 4
 HIGHEST = lax.Precision.HIGHEST
 
 
@@ -204,6 +205,17 @@
     keep.wait()
     for there, other in others():
         e_copy(there, other, there * cores + other).wait_recv()
+
+    early = n - LATE
+
+    def pair_block(t, s):
+        for j in range(windows):
+            w = t * windows + j
+            rows = [left[w, c, 0] * right[c, 0, s] + left[w, c, 1] * right[c, 1, s] for c in range(share)]
+            lagged = jnp.dot(jnp.concatenate(rows, axis=0), table[...], preferred_element_type=jnp.float32)
+            lagged = lagged.reshape(share, windows, LAGS)
+            place = band + windows + s * windows - w
+            part[w, pl.ds(place, windows), :] = jnp.sum(lagged * lagged, axis=0)
 
     def align_step(i, carry):
         t = lax.rem(me + n - i, n)
@@ -239,18 +251,24 @@
                 w = t * windows + j
                 left[w, c, 0] = jnp.concatenate([one_real, -one_real], axis=1).astype(jnp.bfloat16)
                 left[w, c, 1] = jnp.concatenate([one_imag, one_imag], axis=1).astype(jnp.bfloat16)
+
+        def known_pair(k, held):
+            other = lax.rem(me + n - k, n)
+            upper, lower = jnp.maximum(t, other), jnp.minimum(t, other)
+
+            @pl.when(upper - lower <= SPAN)
+            def _():
+                pair_block(upper, lower)
+
+            return held
+
+        @pl.when(i < early)
+        def _():
+            lax.fori_loop(0, i + 1, known_pair, 0)
+
         return carry
 
     lax.fori_loop(0, n, align_step, 0)
-
-    def pair_block(t, s):
-        for j in range(windows):
-            w = t * windows + j
-            rows = [left[w, c, 0] * right[c, 0, s] + left[w, c, 1] * right[c, 1, s] for c in range(share)]
-            lagged = jnp.dot(jnp.concatenate(rows, axis=0), table[...], preferred_element_type=jnp.float32)
-            lagged = lagged.reshape(share, windows, LAGS)
-            place = band + windows + s * windows - w
-            part[w, pl.ds(place, windows), :] = jnp.sum(lagged * lagged, axis=0)
 
     def h_copy(t):
         return pltpu.make_async_remote_copy(
@@ -280,7 +298,12 @@
         t = lax.rem(me + 1 + i, n)
 
         def one_block(s, held):
-            pair_block(t, s)
+            behind = jnp.maximum(lax.rem(me - t + n, n), lax.rem(me - s + n, n))
+
+            @pl.when(behind >= early)
+            def _():
+                pair_block(t, s)
+
             return held
 
         lax.fori_loop(jnp.maximum(t - SPAN, 0), t + 1, one_block, 0)

time: 39.7 us -> 38.9 us (0.980)
  Pallas kernels: 38 us -> 36.9 us
    pallas_call x1, Pallas kernels: 38 us -> 36.9 us  [spread_shards(): pl.pallas_call(functools.partial(kernel, n, chans, windows, share, freq_b...]
where the time goes in v4:
time: 38.9 us; the launch traced here: 38.5 us
  Pallas kernels  36.9 us (95%)
  local copies, waits for them, and re-layouts  1.54 us (4%)
    pallas_call x1, Pallas kernels, spread_shards(): pl.pallas_call(functools.partial(kernel, n, chans, windows, share, freq_b...  36.9 us
    unnamed x1, local copies, waits for them, and re-layouts  1.54 us

profile of v4, /device:TPU:0, one launch (start us, length us, event | category | flops | bytes accessed | tf_op | source)
XLA Modules:
  0.0 38.5 jit_solution(14963574788099180043)
XLA Ops:
  0.0 36.9 %shard_map.37 = f32[4,48,128]{2,1,0:T(8,128)} custom-call(bf16[8,256,128]{2,1,0:T(8,128)(2,1)} %bitcast.2, s32[8]{0:T(128)} %off_ref.1, s32[1,128]{1,0:T(1,128)} %bitcast.3), custom_call_target="tpu_custom_call" | custom-call | tf_op jit(solution)/shard_map/pallas_call | solution.py:348
  36.9 1.5 %copy.5 = f32[4,48,128]{2,1,0:T(8,128)} copy(f32[4,48,128]{2,1,0:T(8,128)} %shard_map.37) | data formatting | bytes 196608
